TPU v7x, 32 devices: a whole 2x2x4 slice. The times are simulated.
32 devices in a mesh: pair: 16 (over z, y, x), dp: 2 (over core).
Axes of the slice: x: 2, y: 2, z: 4, core: 2. Of those that a mesh axis runs over, the one named last changes fastest.
Arguments:
- features: bfloat16 [16384, 2048], P(('pair', 'dp')), may hold values from -6 to 6
- proj_weight: bfloat16 [2048, 128], replicated, may hold values from -0.01171875 to 0.01171875
- row_lse: bfloat16 [16384], P(('pair', 'dp')), may hold values from 6 to 9
- positive: int32 [16384], P(('pair', 'dp')), may hold values from 0 to 16383, as said below
Outputs:
- grad_embed: float32 [16384, 128], P(('pair', 'dp'))
- grad_weight: float32 [2048, 128], P('dp')
Inputs may be any that keep to these rules, and one draw needn't show every extreme that they name: positive[i] names the row that holds the other view of row i's cutout: positive[positive[i]] = i and positive[i] != i.
All inputs are finite; a program needn't handle non-finite values.
Results may differ from a plain program's by a relative error of at most 0.0045.
Values may be sent and summed in bfloat16 or wider, within the bound.
No kernel may reach another device: no remote copies, remote signals or barrier semaphores. Data moves between devices by JAX's collectives and lax.ppermute only.
A program may use at most 64 MiB of HBM per device.

v0:
```python
import jax
import jax.numpy as jnp
from jax import lax
from jax.sharding import PartitionSpec as P

contrastive_divisor = 0.1
epsilon = 1e-06


def from_behind(value, axis, steps):
    count = lax.axis_size(axis)
    pairs = [(source, (source + steps) % count) for source in range(count)]
    return lax.ppermute(value, axis, pairs)


def coupling_tile(embedded, own_lse, own_positive, counterpart_feature_vectors, part_lse, first_id):
    cosine_affinity_matrix = (
        lax.dot_general(
            embedded,
            counterpart_feature_vectors,
            (((1,), (1,)), ((), ())),
            preferred_element_type=jnp.float32,
        )
        / contrastive_divisor
    )
    weights = jnp.exp(cosine_affinity_matrix - own_lse.astype(jnp.float32)[:, None]) + jnp.exp(
        cosine_affinity_matrix - part_lse.astype(jnp.float32)[None, :]
    )
    identity_rows = first_id + jnp.arange(counterpart_feature_vectors.shape[0], dtype=jnp.int32)
    matched = (own_positive[:, None] == identity_rows[None, :]).astype(jnp.float32)
    return (weights - 2.0 * matched).astype(jnp.bfloat16)


def body(features, proj_weight, row_lse, positive):
    row_count = features.shape[0]
    dp_count = lax.axis_size("dp")
    pair_count = lax.axis_size("pair")
    group_rows = row_count * dp_count
    far_offset = pair_count // 4
    my_block = lax.axis_index("pair")
    projected = jnp.dot(features, proj_weight, preferred_element_type=jnp.float32)
    magnitude = jnp.sqrt(jnp.sum(projected * projected, axis=-1, keepdims=True) + epsilon)
    unit_vectors = projected / magnitude
    embedded = unit_vectors.astype(jnp.bfloat16)
    whole_embed, whole_lse = (
        lax.all_gather(embedded, "dp", axis=0, tiled=True),
        lax.all_gather(row_lse, "dp", axis=0, tiled=True),
    )
    upstream_derivative = jnp.zeros((row_count, embedded.shape[1]), jnp.float32)
    for offset in (1, far_offset):
        counterpart_feature_vectors, part_lse = from_behind(
            (whole_embed, whole_lse), "pair", offset
        )
        part_block = jnp.remainder(my_block - offset, pair_count)
        tile_coupling = coupling_tile(
            embedded,
            row_lse,
            positive,
            counterpart_feature_vectors,
            part_lse,
            part_block * group_rows,
        )
        coupling, counterpart_feature_vectors = (tile_coupling, counterpart_feature_vectors)
        upstream_derivative = upstream_derivative + jnp.dot(
            coupling, counterpart_feature_vectors, preferred_element_type=jnp.float32
        )
        returned = lax.psum_scatter(
            lax.dot_general(
                coupling, embedded, (((0,), (0,)), ((), ())), preferred_element_type=jnp.float32
            ),
            "dp",
            scatter_dimension=0,
            tiled=True,
        )
        upstream_derivative = upstream_derivative + from_behind(returned, "pair", -offset)
    derivative_pair_affinity = upstream_derivative / contrastive_divisor
    grad_embed = (
        derivative_pair_affinity
        - unit_vectors * jnp.sum(unit_vectors * derivative_pair_affinity, axis=-1, keepdims=True)
    ) / magnitude
    grad_half = grad_embed.astype(jnp.bfloat16)
    local_term = lax.dot_general(
        features, grad_half, (((0,), (0,)), ((), ())), preferred_element_type=jnp.float32
    )
    summed = lax.psum(local_term, "pair")
    grad_weight = lax.psum_scatter(summed, "dp", scatter_dimension=0, tiled=True)
    return (grad_embed, grad_weight)


def solution(mesh):
    return jax.shard_map(
        body,
        mesh=mesh,
        in_specs=(P(("pair", "dp"), None), P(), P(("pair", "dp")), P(("pair", "dp"))),
        out_specs=(P(("pair", "dp"), None), P("dp", None)),
        check_vma=False,
    )
```

profile of v0, /device:TPU:0, one launch (start us, length us, event | category | flops | bytes accessed | tf_op | source)
XLA Modules:
  0.0 204.0 jit_solution(16239086399272684663)
XLA Ops:
  7.2 0.0 copy-start
  7.2 0.0 copy-start.4
  7.2 0.0 reduce-scatter.6.cloned.1.call-start
  7.2 1.5 copy-done
  8.8 1.9 multiply_reduce_fusion.1
  10.6 0.0 copy-start.5
  10.7 2.1 %all_gather.6 = bf16[1024,128]{0,1:T(8,128)(2,1)S(1)} all-gather(bf16[512,128]{0,1:T(8,128)(2,1)S(1)} %fusion.4), channel_id=1, replica_groups=mesh['pair'=16,'dp'=2] {'dp'}, dimensions={0}, use_global_device_ids=true | all-gather | bytes 393216 | tf_op jit(solution)/shard_map/all_gather | solution.py:46
  12.8 2.9 %collective-permute-start.3 = (bf16[1024,128]{0,1:T(8,128)(2,1)S(1)}, bf16[1024,128]{0,1:T(8,128)(2,1)S(1)}, u32[]{:S(2)}, u32[]{:S(2)}) collective-permute-start(bf16[1024,128]{0,1:T(8,128)(2,1)S(1)} %all_gather.6), channel_id=1, source_target_pairs={{0,8},{2,10},{4,12},{6,14},{8,16},{10,18},{12,20},{14,22},{16,24},... | collective-permute-start | bytes 786440 | tf_op jit(solution)/shard_map/ppermute | solution.py:13
  15.7 0.0 copy-done.4
  15.7 1.8 all-gather
  17.5 1.6 collective-permute-start.4
  19.2 1.5 collective-permute-start.1
  20.7 1.5 collective-permute-start
  22.1 2.3 %collective-permute-done.4 = bf16[1024]{0:T(1024)(128)(2,1)S(1)} collective-permute-done((bf16[1024]{0:T(1024)(128)(2,1)S(1)}, bf16[1024]{0:T(1024)(128)(2,1)S(1)}, u32[]{:S(2)}, u32[]{:S(2)}) %collective-permute-start.4) | collective-permute-done | bytes 2080 | tf_op jit(solution)/shard_map/ppermute | solution.py:13
  24.4 1.9 collective-permute-done.1
  26.3 0.0 collective-permute-done.3
  26.3 0.0 copy-start.2
  26.4 0.5 fusion.5
  26.8 5.3 %collective-permute-done = bf16[1024,128]{0,1:T(8,128)(2,1)S(1)} collective-permute-done((bf16[1024,128]{0,1:T(8,128)(2,1)S(1)}, bf16[1024,128]{0,1:T(8,128)(2,1)S(1)}, u32[]{:S(2)}, u32[]{:S(2)}) %collective-permute-start) | collective-permute-done | bytes 262176 | tf_op jit(solution)/shard_map/ppermute | solution.py:13
  32.1 0.0 copy-start.3
  32.1 0.0 copy-done.2
  32.1 0.7 copy-done.3
  32.8 0.0 copy-done.5
  32.8 3.0 %subtract_convert_fusion.1 = (bf16[512,1024]{1,0:T(8,128)(2,1)S(1)}, bf16[512,1024]{1,0:T(8,128)(2,1)S(1)}) fusion(s32[1024]{0:T(1024)S(1)} %get-tuple-element.15, f32[1024]{0:T(1024)S(1)} %convert_element_type.26, f32[512]{0:T(512)S(1)} %convert_element_type.25, s32[512]{0:T(512)S(1)} %copy-done.5, s32[1024]{0:T(1024)S(1)} %get-tuple-element.14, ...), kind=kOutput, calls=%fused_computation.2 | convolution fusion | flops 142606336 | bytes 4608000 | tf_op jit(solution)/shard_map/dot_general | solution.py:18
  35.8 0.0 copy-start.1
  35.8 1.0 copy-done.1
  36.7 1.1 fusion.8
  37.9 0.0 reduce-scatter.6.cloned.1.call-update
  37.9 0.0 reduce-scatter.4.cloned.1.call-start
  37.9 1.1 fusion.7
  39.1 0.0 reduce-scatter.4.cloned.1.call-update
  39.1 0.0 reduce-scatter.8.cloned.1.call-start
  39.1 4.2 %reduce-scatter.6.cloned.1.call-done = f32[512,128]{0,1:T(8,128)} async-done(((f32[1024,128]{0,1:T(8,128)}), f32[512,128]{0,1:T(8,128)}) %reduce-scatter.6.cloned.1.call-update) | async-done | bytes 262160 | tf_op jit(solution)/shard_map/reduce_scatter | solution.py:67
  43.4 3.6 %collective-permute-start.5 = (f32[512,128]{0,1:T(8,128)}, f32[512,128]{0,1:T(8,128)}, u32[]{:S(2)}, u32[]{:S(2)}) collective-permute-start(f32[512,128]{0,1:T(8,128)} %reduce-scatter.6.cloned.1.call-done), channel_id=1, source_target_pairs={{0,24},{2,26},{4,28},{6,30},{8,0},{10,2},{12,4},{14,6},{16,8},{18,... | collective-permute-start | bytes 786440 | tf_op jit(solution)/shard_map/ppermute | solution.py:13
  46.9 7.9 %reduce-scatter.4.cloned.1.call-done = f32[512,128]{0,1:T(8,128)} async-done(((f32[1024,128]{0,1:T(8,128)}), f32[512,128]{0,1:T(8,128)}) %reduce-scatter.4.cloned.1.call-update) | async-done | bytes 262160 | tf_op jit(solution)/shard_map/reduce_scatter | solution.py:67
  54.8 5.4 %collective-permute-start.2 = (f32[512,128]{0,1:T(8,128)}, f32[512,128]{0,1:T(8,128)S(1)}, u32[]{:S(2)}, u32[]{:S(2)}) collective-permute-start(f32[512,128]{0,1:T(8,128)} %reduce-scatter.4.cloned.1.call-done), channel_id=1, source_target_pairs={{0,30},{2,0},{4,2},{6,4},{8,6},{10,8},{12,10},{14,12},{16,14},{18,... | collective-permute-start | bytes 786440 | tf_op jit(solution)/shard_map/ppermute | solution.py:13
  60.2 1.7 fusion.6
  62.0 0.0 collective-permute-done.5
  62.0 4.6 %collective-permute-done.2 = f32[512,128]{0,1:T(8,128)S(1)} collective-permute-done((f32[512,128]{0,1:T(8,128)}, f32[512,128]{0,1:T(8,128)S(1)}, u32[]{:S(2)}, u32[]{:S(2)}) %collective-permute-start.2) | collective-permute-done | bytes 262176 | tf_op jit(solution)/shard_map/ppermute | solution.py:13
  66.6 1.6 multiply_reduce_fusion
  68.1 0.1 subtract_divide_fusion
  68.2 1.4 convolution_bitcast_fusion
  69.6 0.0 reduce-scatter.8.cloned.1.call-update
  69.6 0.0 all-reduce.2.cloned.1.call-start
  69.7 10.4 %reduce-scatter.8.cloned.1.call-done = f32[1024,128]{0,1:T(8,128)} async-done(((f32[2048,128]{0,1:T(8,128)}), f32[1024,128]{0,1:T(8,128)}) %reduce-scatter.8.cloned.1.call-update) | async-done | bytes 524304 | tf_op jit(solution)/shard_map/reduce_scatter | solution.py:86
  80.1 0.0 all-reduce.2.cloned.1.call-update
  80.1 0.8 copy.16
  80.9 114.5 %all-reduce.2.cloned.1.call-done = f32[1024,128]{0,1:T(8,128)} async-done(((f32[1024,128]{0,1:T(8,128)}), f32[1024,128]{0,1:T(8,128)}) %all-reduce.2.cloned.1.call-update) | async-done | bytes 524304 | tf_op jit(solution)/shard_map/psum | solution.py:85
  195.4 2.0 copy.17
  (9 shorter events, 0.1 us)
Async XLA Ops:
  7.2 1.6 copy-start
  7.2 8.5 %copy-start.4 = (bf16[512]{0:T(512)(128)(2,1)S(1)}, bf16[512]{0:T(512)(128)(2,1)}, u32[]{:S(2)}) copy-start(bf16[512]{0:T(512)(128)(2,1)} %param.6) | copy-start | bytes 3076
  7.2 36.2 %reduce-scatter.6.cloned.1.call-start = ((), (), s32[]{:S(2)}) async-start(), calls=%async_computation.4 | async-start | bytes 786432 | tf_op jit(solution)/shard_map/reduce_scatter | solution.py:67
  10.6 22.2 %copy-start.5 = (s32[512]{0:T(512)S(1)}, s32[512]{0:T(512)}, u32[]{:S(2)}) copy-start(s32[512]{0:T(512)} %param.7) | copy-start | bytes 6148
  12.8 13.6 %collective-permute-start.3 = (bf16[1024,128]{0,1:T(8,128)(2,1)S(1)}, bf16[1024,128]{0,1:T(8,128)(2,1)S(1)}, u32[]{:S(2)}, u32[]{:S(2)}) collective-permute-start(bf16[1024,128]{0,1:T(8,128)(2,1)S(1)} %all_gather.6), channel_id=1, source_target_pairs={{0,8},{2,10},{4,12},{6,14},{8,16},{10,18},{12,20},{14,22},{16,24},... | collective-permute-start | bytes 786440 | tf_op jit(solution)/shard_map/ppermute | solution.py:13
  17.5 6.9 %collective-permute-start.4 = (bf16[1024]{0:T(1024)(128)(2,1)S(1)}, bf16[1024]{0:T(1024)(128)(2,1)S(1)}, u32[]{:S(2)}, u32[]{:S(2)}) collective-permute-start(bf16[1024]{0:T(1024)(128)(2,1)S(1)} %bitcast.20), channel_id=1, source_target_pairs={{0,8},{2,10},{4,12},{6,14},{8,16},{10,18},{12,20},{14,22},{16,24},... | collective-permute-start | bytes 6152 | tf_op jit(solution)/shard_map/ppermute | solution.py:13
  19.2 7.2 %collective-permute-start.1 = (bf16[1024]{0:T(1024)(128)(2,1)S(1)}, bf16[1024]{0:T(1024)(128)(2,1)S(1)}, u32[]{:S(2)}, u32[]{:S(2)}) collective-permute-start(bf16[1024]{0:T(1024)(128)(2,1)S(1)} %bitcast.21), channel_id=1, source_target_pairs={{0,2},{2,4},{4,6},{6,8},{8,10},{10,12},{12,14},{14,16},{16,18},{18... | collective-permute-start | bytes 6152 | tf_op jit(solution)/shard_map/ppermute | solution.py:13
  20.7 11.5 %collective-permute-start = (bf16[1024,128]{0,1:T(8,128)(2,1)S(1)}, bf16[1024,128]{0,1:T(8,128)(2,1)S(1)}, u32[]{:S(2)}, u32[]{:S(2)}) collective-permute-start(bf16[1024,128]{0,1:T(8,128)(2,1)S(1)} %all_gather.6), channel_id=1, source_target_pairs={{0,2},{2,4},{4,6},{6,8},{8,10},{10,12},{12,14},{14,16},{16,18},{18... | collective-permute-start | bytes 786440 | tf_op jit(solution)/shard_map/ppermute | solution.py:13
  26.3 5.8 %copy-start.2 = (bf16[1024,128]{0,1:T(8,128)(2,1)}, bf16[1024,128]{0,1:T(8,128)(2,1)S(1)}, u32[]{:S(2)}) copy-start(bf16[1024,128]{0,1:T(8,128)(2,1)S(1)} %collective-permute-done.3) | copy-start | bytes 786436
  32.1 0.7 copy-start.3
  35.8 1.0 copy-start.1
  37.9 17.0 %reduce-scatter.4.cloned.1.call-start = ((), (), s32[]{:S(2)}) async-start(), calls=%async_computation.3 | async-start | bytes 786432 | tf_op jit(solution)/shard_map/reduce_scatter | solution.py:67
  39.1 41.0 %reduce-scatter.8.cloned.1.call-start = ((), (), s32[]{:S(2)}) async-start(), calls=%async_computation.5 | async-start | bytes 1572864 | tf_op jit(solution)/shard_map/reduce_scatter | solution.py:86
  43.4 18.6 %collective-permute-start.5 = (f32[512,128]{0,1:T(8,128)}, f32[512,128]{0,1:T(8,128)}, u32[]{:S(2)}, u32[]{:S(2)}) collective-permute-start(f32[512,128]{0,1:T(8,128)} %reduce-scatter.6.cloned.1.call-done), channel_id=1, source_target_pairs={{0,24},{2,26},{4,28},{6,30},{8,0},{10,2},{12,4},{14,6},{16,8},{18,... | collective-permute-start | bytes 786440 | tf_op jit(solution)/shard_map/ppermute | solution.py:13
  54.8 11.7 %collective-permute-start.2 = (f32[512,128]{0,1:T(8,128)}, f32[512,128]{0,1:T(8,128)S(1)}, u32[]{:S(2)}, u32[]{:S(2)}) collective-permute-start(f32[512,128]{0,1:T(8,128)} %reduce-scatter.4.cloned.1.call-done), channel_id=1, source_target_pairs={{0,30},{2,0},{4,2},{6,4},{8,6},{10,8},{12,10},{14,12},{16,14},{18,... | collective-permute-start | bytes 786440 | tf_op jit(solution)/shard_map/ppermute | solution.py:13
  69.6 125.8 %all-reduce.2.cloned.1.call-start = ((), (), s32[]{:S(2)}) async-start(), calls=%async_computation.6 | async-start | bytes 1048576 | tf_op jit(solution)/shard_map/psum | solution.py:85
Sparse Core Ops, SparseCore 0:
  38.0 5.3 reduce-scatter.5
  45.7 9.1 reduce-scatter.3
  69.8 10.2 reduce-scatter.7
  85.9 109.4 all-reduce.1
where the time goes:
time: 204 us
  waiting for transfers between devices  151 us (74%)
  starting transfers between devices  16.6 us (8%)
  between operations  13.9 us (7%)
  matrix products  12.2 us (6%)
  local copies, waits for them, and re-layouts  6.09 us (3%)
  blocking collectives  3.86 us (2%)
    psum x1, waiting for transfers between devices, body(): summed = lax.psum(local_term, 'pair')  114 us
    ppermute x6, starting transfers between devices, from_behind(): return lax.ppermute(value, axis, pairs)  16.5 us
    ppermute x6, waiting for transfers between devices, from_behind(): return lax.ppermute(value, axis, pairs)  14.1 us
    reduce_scatter x2, waiting for transfers between devices, body(): lax.psum_scatter(lax.dot_general(coupling, embedded, (((0,), (0,)), ((),...  12.2 us
    reduce_scatter x1, waiting for transfers between devices, body(): lax.psum_scatter(summed, 'dp', scatter_dimension=0, tiled=True)  10.4 us
    unnamed x16, local copies, waits for them, and re-layouts  6.09 us
  transfers between devices with their start and end apart: 10, of which 8 were waited for; matrix products, arithmetic and copies ran while one was open for 2% of the time, Pallas kernels for 0%

commit v1 on v0

--- a/solution.py
+++ b/solution.py
@@ -82,7 +82,7 @@
     local_term = lax.dot_general(
         features, grad_half, (((0,), (0,)), ((), ())), preferred_element_type=jnp.float32
     )
-    summed = lax.psum(local_term, "pair")
+    summed = jnp.sum(lax.all_gather(local_term, "pair"), axis=0)
     grad_weight = lax.psum_scatter(summed, "dp", scatter_dimension=0, tiled=True)
     return (grad_embed, grad_weight)
 

time: 204 us -> 308 us (1.51)
  waiting for transfers between devices: 151 us -> 226 us
  local copies, waits for them, and re-layouts: 6.09 us -> 23.8 us
  other arithmetic: 0.13 us -> 10.7 us
    all_gather x0 -> x1, waiting for transfers between devices: none -> 193 us  [body(): summed = jnp.sum(lax.all_gather(local_term, 'pair'), axis=0)]
    psum x1 -> x0, waiting for transfers between devices: 114 us -> none  [body(): summed = lax.psum(local_term, 'pair')]
    unnamed x16 -> x17, local copies, waits for them, and re-layouts: 6.09 us -> 23.8 us
    reduce_sum x0 -> x1, other arithmetic: none -> 10.6 us  [body(): summed = jnp.sum(lax.all_gather(local_term, 'pair'), axis=0)]
    reduce_scatter x1, waiting for transfers between devices: 10.4 us -> 7.01 us  [body(): lax.psum_scatter(summed, 'dp', scatter_dimension=0, tiled=True)]
  transfers between devices with their start and end apart: 10 -> 10, of which waited for: 8 -> 8; matrix products, arithmetic and copies ran while one was open for 2% -> 1% of each run, Pallas kernels for 0% -> 0%
where the time goes in v1:
time: 308 us; the launch traced here: 307 us
  waiting for transfers between devices  226 us (73%)
  local copies, waits for them, and re-layouts  23.8 us (8%)
  starting transfers between devices  16.8 us (5%)
  between operations  13.9 us (5%)
  matrix products  12.3 us (4%)
  other arithmetic  10.7 us (3%)
  blocking collectives  3.85 us (1%)
    all_gather x1, waiting for transfers between devices, body(): summed = jnp.sum(lax.all_gather(local_term, 'pair'), axis=0)  193 us
    unnamed x17, local copies, waits for them, and re-layouts  23.8 us
    ppermute x6, starting transfers between devices, from_behind(): return lax.ppermute(value, axis, pairs)  16.5 us
    ppermute x6, waiting for transfers between devices, from_behind(): return lax.ppermute(value, axis, pairs)  14.1 us
    reduce_scatter x2, waiting for transfers between devices, body(): lax.psum_scatter(lax.dot_general(coupling, embedded, (((0,), (0,)), ((),...  12.1 us
    reduce_sum x1, other arithmetic, body(): summed = jnp.sum(lax.all_gather(local_term, 'pair'), axis=0)  10.6 us
    reduce_scatter x1, waiting for transfers between devices, body(): lax.psum_scatter(summed, 'dp', scatter_dimension=0, tiled=True)  7.01 us
  transfers between devices with their start and end apart: 10, of which 8 were waited for; matrix products, arithmetic and copies ran while one was open for 1% of the time, Pallas kernels for 0%

profile of v1, /device:TPU:0, one launch (start us, length us, event | category | flops | bytes accessed | tf_op | source)
XLA Modules:
  0.0 307.3 jit_solution(11187594088524713232)
XLA Ops:
  7.2 0.0 copy-start
  7.2 0.0 copy-start.4
  7.2 0.0 reduce-scatter.6.cloned.1.call-start
  7.2 1.5 copy-done
  8.8 1.9 multiply_reduce_fusion.1
  10.6 0.0 copy-start.5
  10.7 2.1 all_gather.12
  12.8 2.9 collective-permute-start.3
  15.7 0.0 copy-done.4
  15.7 1.8 all-gather.1
  17.5 1.6 collective-permute-start.4
  19.2 1.5 collective-permute-start.1
  20.7 1.5 collective-permute-start
  22.1 2.3 collective-permute-done.4
  24.4 1.9 collective-permute-done.1
  26.3 0.0 collective-permute-done.3
  26.3 0.0 copy-start.2
  26.4 0.5 fusion.5
  26.8 5.3 %collective-permute-done = bf16[1024,128]{0,1:T(8,128)(2,1)S(1)} collective-permute-done((bf16[1024,128]{0,1:T(8,128)(2,1)S(1)}, bf16[1024,128]{0,1:T(8,128)(2,1)S(1)}, u32[]{:S(2)}, u32[]{:S(2)}) %collective-permute-start) | collective-permute-done | bytes 262176 | tf_op jit(solution)/shard_map/ppermute | solution.py:13
  32.1 0.0 copy-start.3
  32.1 0.0 copy-done.2
  32.1 0.7 copy-done.3
  32.8 0.0 copy-done.5
  32.8 3.0 subtract_convert_fusion.1
  35.8 0.0 copy-start.1
  35.8 1.0 copy-done.1
  36.8 1.1 fusion.8
  37.9 0.0 reduce-scatter.6.cloned.1.call-update
  37.9 0.0 reduce-scatter.4.cloned.1.call-start
  37.9 1.1 fusion.7
  39.1 0.0 reduce-scatter.4.cloned.1.call-update
  39.1 0.0 all-gather.4.cloned.1.call-start
  39.1 4.2 %reduce-scatter.6.cloned.1.call-done = f32[512,128]{0,1:T(8,128)} async-done(((f32[1024,128]{0,1:T(8,128)}), f32[512,128]{0,1:T(8,128)}) %reduce-scatter.6.cloned.1.call-update) | async-done | bytes 262160 | tf_op jit(solution)/shard_map/reduce_scatter | solution.py:67
  43.4 3.6 %collective-permute-start.5 = (f32[512,128]{0,1:T(8,128)}, f32[512,128]{0,1:T(8,128)}, u32[]{:S(2)}, u32[]{:S(2)}) collective-permute-start(f32[512,128]{0,1:T(8,128)} %reduce-scatter.6.cloned.1.call-done), channel_id=1, source_target_pairs={{0,24},{2,26},{4,28},{6,30},{8,0},{10,2},{12,4},{14,6},{16,8},{18,... | collective-permute-start | bytes 786440 | tf_op jit(solution)/shard_map/ppermute | solution.py:13
  46.9 7.9 %reduce-scatter.4.cloned.1.call-done = f32[512,128]{0,1:T(8,128)} async-done(((f32[1024,128]{0,1:T(8,128)}), f32[512,128]{0,1:T(8,128)}) %reduce-scatter.4.cloned.1.call-update) | async-done | bytes 262160 | tf_op jit(solution)/shard_map/reduce_scatter | solution.py:67
  54.8 5.4 %collective-permute-start.2 = (f32[512,128]{0,1:T(8,128)}, f32[512,128]{0,1:T(8,128)S(1)}, u32[]{:S(2)}, u32[]{:S(2)}) collective-permute-start(f32[512,128]{0,1:T(8,128)} %reduce-scatter.4.cloned.1.call-done), channel_id=1, source_target_pairs={{0,30},{2,0},{4,2},{6,4},{8,6},{10,8},{12,10},{14,12},{16,14},{18,... | collective-permute-start | bytes 786440 | tf_op jit(solution)/shard_map/ppermute | solution.py:13
  60.2 1.7 fusion.6
  61.9 0.0 collective-permute-done.5
  62.0 4.6 %collective-permute-done.2 = f32[512,128]{0,1:T(8,128)S(1)} collective-permute-done((f32[512,128]{0,1:T(8,128)}, f32[512,128]{0,1:T(8,128)S(1)}, u32[]{:S(2)}, u32[]{:S(2)}) %collective-permute-start.2) | collective-permute-done | bytes 262176 | tf_op jit(solution)/shard_map/ppermute | solution.py:13
  66.6 1.6 multiply_reduce_fusion
  68.1 0.1 subtract_divide_fusion
  68.2 1.4 convolution_bitcast_fusion
  69.6 0.0 all-gather.4.cloned.1.call-update
  69.6 0.2 reduce-scatter.8.cloned.1.call-start
  69.9 192.7 %all-gather.4.cloned.1.call-done = f32[32768,128]{0,1:T(8,128)} async-done(((f32[2048,128]{0,1:T(8,128)}), f32[32768,128]{0,1:T(8,128)}) %all-gather.4.cloned.1.call-update) | async-done | bytes 16777232 | tf_op jit(solution)/shard_map/all_gather | solution.py:85
  262.6 17.7 %copy.19 = f32[16,8,16,2048]{3,2,1,0:T(8,128)} copy(f32[16,8,16,2048]{3,1,2,0:T(8,128)} %bitcast.24) | data formatting | bytes 33554432
  280.3 10.6 %bitcast_reduce_fusion = f32[2048,128]{0,1:T(8,128)} fusion(f32[16,8,16,2048]{3,2,1,0:T(8,128)} %copy.19), kind=kLoop, calls=%fused_computation | loop fusion | flops 3932160 | bytes 17825792 | tf_op jit(solution)/shard_map/reduce_sum | solution.py:85
  290.9 0.0 reduce-scatter.8.cloned.1.call-update
  290.9 0.8 copy.14
  291.8 7.0 %reduce-scatter.8.cloned.1.call-done = f32[1024,128]{0,1:T(8,128)} async-done(((f32[2048,128]{0,1:T(8,128)}), f32[1024,128]{0,1:T(8,128)}) %reduce-scatter.8.cloned.1.call-update) | async-done | bytes 524304 | tf_op jit(solution)/shard_map/reduce_scatter | solution.py:86
  298.8 2.0 copy.15
  (9 shorter events, 0.1 us)
Async XLA Ops:
  7.2 1.6 copy-start
  7.2 8.5 %copy-start.4 = (bf16[512]{0:T(512)(128)(2,1)S(1)}, bf16[512]{0:T(512)(128)(2,1)}, u32[]{:S(2)}) copy-start(bf16[512]{0:T(512)(128)(2,1)} %param.6) | copy-start | bytes 3076
  7.2 36.2 %reduce-scatter.6.cloned.1.call-start = ((), (), s32[]{:S(2)}) async-start(), calls=%async_computation.4 | async-start | bytes 786432 | tf_op jit(solution)/shard_map/reduce_scatter | solution.py:67
  10.6 22.2 %copy-start.5 = (s32[512]{0:T(512)S(1)}, s32[512]{0:T(512)}, u32[]{:S(2)}) copy-start(s32[512]{0:T(512)} %param.7) | copy-start | bytes 6148
  12.8 13.6 %collective-permute-start.3 = (bf16[1024,128]{0,1:T(8,128)(2,1)S(1)}, bf16[1024,128]{0,1:T(8,128)(2,1)S(1)}, u32[]{:S(2)}, u32[]{:S(2)}) collective-permute-start(bf16[1024,128]{0,1:T(8,128)(2,1)S(1)} %all_gather.12), channel_id=1, source_target_pairs={{0,8},{2,10},{4,12},{6,14},{8,16},{10,18},{12,20},{14,22},{16,24},... | collective-permute-start | bytes 786440 | tf_op jit(solution)/shard_map/ppermute | solution.py:13
  17.5 6.9 %collective-permute-start.4 = (bf16[1024]{0:T(1024)(128)(2,1)S(1)}, bf16[1024]{0:T(1024)(128)(2,1)S(1)}, u32[]{:S(2)}, u32[]{:S(2)}) collective-permute-start(bf16[1024]{0:T(1024)(128)(2,1)S(1)} %bitcast.26), channel_id=1, source_target_pairs={{0,8},{2,10},{4,12},{6,14},{8,16},{10,18},{12,20},{14,22},{16,24},... | collective-permute-start | bytes 6152 | tf_op jit(solution)/shard_map/ppermute | solution.py:13
  19.2 7.2 %collective-permute-start.1 = (bf16[1024]{0:T(1024)(128)(2,1)S(1)}, bf16[1024]{0:T(1024)(128)(2,1)S(1)}, u32[]{:S(2)}, u32[]{:S(2)}) collective-permute-start(bf16[1024]{0:T(1024)(128)(2,1)S(1)} %bitcast.27), channel_id=1, source_target_pairs={{0,2},{2,4},{4,6},{6,8},{8,10},{10,12},{12,14},{14,16},{16,18},{18... | collective-permute-start | bytes 6152 | tf_op jit(solution)/shard_map/ppermute | solution.py:13
  20.7 11.5 %collective-permute-start = (bf16[1024,128]{0,1:T(8,128)(2,1)S(1)}, bf16[1024,128]{0,1:T(8,128)(2,1)S(1)}, u32[]{:S(2)}, u32[]{:S(2)}) collective-permute-start(bf16[1024,128]{0,1:T(8,128)(2,1)S(1)} %all_gather.12), channel_id=1, source_target_pairs={{0,2},{2,4},{4,6},{6,8},{8,10},{10,12},{12,14},{14,16},{16,18},{18... | collective-permute-start | bytes 786440 | tf_op jit(solution)/shard_map/ppermute | solution.py:13
  26.3 5.8 %copy-start.2 = (bf16[1024,128]{0,1:T(8,128)(2,1)}, bf16[1024,128]{0,1:T(8,128)(2,1)S(1)}, u32[]{:S(2)}) copy-start(bf16[1024,128]{0,1:T(8,128)(2,1)S(1)} %collective-permute-done.3) | copy-start | bytes 786436
  32.1 0.7 copy-start.3
  35.8 1.0 copy-start.1
  37.9 16.9 %reduce-scatter.4.cloned.1.call-start = ((), (), s32[]{:S(2)}) async-start(), calls=%async_computation.3 | async-start | bytes 786432 | tf_op jit(solution)/shard_map/reduce_scatter | solution.py:67
  39.1 223.5 %all-gather.4.cloned.1.call-start = ((), (), s32[]{:S(2)}) async-start(), calls=%async_computation.6 | async-start | bytes 17825792 | tf_op jit(solution)/shard_map/all_gather | solution.py:85
  43.4 18.6 %collective-permute-start.5 = (f32[512,128]{0,1:T(8,128)}, f32[512,128]{0,1:T(8,128)}, u32[]{:S(2)}, u32[]{:S(2)}) collective-permute-start(f32[512,128]{0,1:T(8,128)} %reduce-scatter.6.cloned.1.call-done), channel_id=1, source_target_pairs={{0,24},{2,26},{4,28},{6,30},{8,0},{10,2},{12,4},{14,6},{16,8},{18,... | collective-permute-start | bytes 786440 | tf_op jit(solution)/shard_map/ppermute | solution.py:13
  54.8 11.8 %collective-permute-start.2 = (f32[512,128]{0,1:T(8,128)}, f32[512,128]{0,1:T(8,128)S(1)}, u32[]{:S(2)}, u32[]{:S(2)}) collective-permute-start(f32[512,128]{0,1:T(8,128)} %reduce-scatter.4.cloned.1.call-done), channel_id=1, source_target_pairs={{0,30},{2,0},{4,2},{6,4},{8,6},{10,8},{12,10},{14,12},{16,14},{18,... | collective-permute-start | bytes 786440 | tf_op jit(solution)/shard_map/ppermute | solution.py:13
  69.6 229.1 %reduce-scatter.8.cloned.1.call-start = ((), (), s32[]{:S(2)}) async-start(), calls=%async_computation.5 | async-start | bytes 1572864 | tf_op jit(solution)/shard_map/reduce_scatter | solution.py:86
Sparse Core Ops, SparseCore 0:
  38.0 5.3 reduce-scatter.5
  45.7 9.0 reduce-scatter.3
  69.8 192.8 all-gather.3
  291.0 7.6 reduce-scatter.7
